TPU v7x, 256 devices: a whole 4x4x8 slice. The times are simulated.
256 devices in a mesh: stem: 8 (over z_lo, y), tm: 32 (over x, z_hi, core).
Axes of the slice: x: 4, y: 4, z: 8 (z_hi: 4, z_lo: 2; z = z_hi * 2 + z_lo), core: 2. Of those that a mesh axis runs over, the one named last changes fastest.
Arguments:
- frames: bfloat16 [8, 12288, 1024], P('stem', 'tm'), may hold values from -6 to 6
- timestep: int32 [8], replicated, may hold values from 0 to 49, as said below
- modulation: float32 [50, 6, 1024], replicated, may hold values from -3 to 3
- qkv_self: bfloat16 [1024, 1536], replicated, may hold values from -0.1875 to 0.1875
- out_self: bfloat16 [512, 1024], replicated, may hold values from -0.25 to 0.25
- qk_gain_self: float32 [2, 64], replicated, may hold values from 1.5 to 6
- qkv_cross: bfloat16 [1024, 1536], replicated, may hold values from -0.1875 to 0.1875
- out_cross: bfloat16 [512, 1024], replicated, may hold values from -0.25 to 0.25
- qk_gain_cross: float32 [2, 64], replicated, may hold values from 1.5 to 6
Outputs:
- layer_out: bfloat16 [8, 12288, 1024], P('stem', 'tm')
Inputs may be any that keep to these rules, and one draw needn't show every extreme that they name: The stems' timestep indices are distinct, and index 0 and index 49 are always among them.
All inputs are finite; a program needn't handle non-finite values.
Results may differ from a plain program's by a relative error of at most 0.015.
The roundings to bfloat16 on the way count: a program that leaves them out, or rounds other values in their place, can miss the bound.
Values may be sent and summed in bfloat16 or wider, within the bound.
A program may use at most 128 MiB of HBM per device.

v0:
```python
import jax
import jax.numpy as jnp
from jax import lax
from jax.sharding import PartitionSpec as P

D = 1024
H = 8
HD = 64
HALF = 256
EPS = 1e-06
NEG = -1e30


def padded_2(block, sides, width):
    for axis, dim in sides:
        count = lax.axis_size(axis)
        forward = [(i, i + 1) for i in range(count - 1)]
        backward = [(target, source) for source, target in forward]
        low = lax.ppermute(
            lax.slice_in_dim(block, block.shape[dim] - width, None, axis=dim), axis, forward
        )
        high = lax.ppermute(lax.slice_in_dim(block, 0, width, axis=dim), axis, backward)
        block = jnp.concatenate([low, block, high], axis=dim)
    return block


def rounded(values):
    return lax.optimization_barrier(values.astype(jnp.bfloat16))


def layer_norm(values):
    values = values.astype(jnp.float32)
    centred = values - jnp.mean(values, axis=-1, keepdims=True)
    return centred * lax.rsqrt(jnp.mean(centred * centred, axis=-1, keepdims=True) + EPS)


def modulate(values, shift, scale):
    return layer_norm(values) * (1.0 + scale) + shift


def head_norm(values, gain):
    shaped = values.reshape(values.shape[:-1] + (H, HD))
    return shaped * lax.rsqrt(jnp.mean(shaped * shaped, axis=-1, keepdims=True) + EPS) * gain


def split_heads(projected, gains):
    width = H * HD
    query = rounded(head_norm(projected[..., :width], gains[0]))
    keyset = rounded(head_norm(projected[..., width : 2 * width], gains[1]))
    valueset = rounded(projected[..., 2 * width :].reshape(projected.shape[:-1] + (H, HD)))
    return (query, keyset, valueset)


def softmax_rows(scores):
    top = jnp.max(scores, axis=-1, keepdims=True)
    raised = jnp.exp(scores - top)
    return rounded(raised / jnp.sum(raised, axis=-1, keepdims=True))


def window_attend(query, padded, offset, total):
    rows = query.shape[0]
    width = H * HD

    def one_block(index):
        start = index * rows
        k_block = padded[0].reshape(-1, H, HD)
        v_block = padded[1].reshape(-1, H, HD)
        scores = jnp.einsum(
            "qhd,khd->hqk", query, k_block, preferred_element_type=jnp.float32
        ) * HD ** (-0.5)
        q_pos = offset + start + jnp.arange(rows, dtype=jnp.int32)
        k_pos = offset + start - HALF + jnp.arange(rows + 2 * HALF, dtype=jnp.int32)
        keep = (
            (jnp.abs(q_pos[:, None] - k_pos[None, :]) <= HALF)
            & (k_pos[None, :] >= 0)
            & (k_pos[None, :] < total)
        )
        weights = softmax_rows(jnp.where(keep[None], scores, NEG))
        return jnp.einsum("hqk,khd->qhd", weights, v_block, preferred_element_type=jnp.float32)

    blocks = lax.map(one_block, jnp.arange(rows // rows, dtype=jnp.int32))
    return rounded(blocks.reshape(rows, width))


def on_device(
    frames,
    timestep,
    modulation,
    qkv_self,
    out_self,
    qk_gain_self,
    qkv_cross,
    out_cross,
    qk_gain_cross,
):
    stem_count = lax.axis_size("stem")
    time_count = lax.axis_size("tm")
    rows = frames.shape[1]
    width = H * HD
    steps_all = modulation.shape[0]
    picks = (timestep[:, None] == jnp.arange(steps_all, dtype=jnp.int32)[None, :]).astype(
        jnp.float32
    )
    table = jnp.dot(
        picks, modulation.reshape(steps_all, -1), precision=lax.Precision.HIGHEST
    ).reshape(stem_count, 6, D)
    own = lax.dynamic_index_in_dim(table, lax.axis_index("stem"), 0, keepdims=False)
    source = frames[0]
    normed_self = rounded(modulate(source, own[0], own[1]))
    projected = jnp.dot(normed_self, qkv_self, preferred_element_type=jnp.float32)
    query, keyset, valueset = split_heads(projected, qk_gain_self)
    stacked = jnp.stack([keyset.reshape(rows, width), valueset.reshape(rows, width)])
    padded = padded_2(stacked, (("tm", 1),), HALF)
    offset = lax.axis_index("tm") * rows
    attended = window_attend(query, padded, offset, rows * time_count)
    first = rounded(
        source.astype(jnp.float32)
        + own[2] * jnp.dot(attended, out_self, preferred_element_type=jnp.float32)
    )
    normed_cross = rounded(modulate(first, own[3], own[4]))
    projected_cross = jnp.dot(normed_cross, qkv_cross, preferred_element_type=jnp.float32)
    q_cross, k_cross, v_cross = split_heads(projected_cross, qk_gain_cross)
    pair = jnp.stack([k_cross.reshape(rows, width), v_cross.reshape(rows, width)])[None]
    every = lax.all_gather(pair, "stem", axis=0, tiled=True)
    k_all = every[:, 0].reshape(stem_count, rows, H, HD)
    v_all = every[:, 1].reshape(stem_count, rows, H, HD)
    scores = jnp.einsum(
        "fhd,tfhd->fht", q_cross, k_all, preferred_element_type=jnp.float32
    ) * HD ** (-0.5)
    weights = softmax_rows(scores)
    mixed = rounded(
        jnp.einsum("fht,tfhd->fhd", weights, v_all, preferred_element_type=jnp.float32)
    ).reshape(rows, width)
    cross_out = rounded(jnp.dot(mixed, out_cross, preferred_element_type=jnp.float32))
    result = (first.astype(jnp.float32) + own[5] * cross_out.astype(jnp.float32)).astype(
        jnp.bfloat16
    )
    return result[None]


def solution(mesh):
    return jax.shard_map(
        on_device,
        mesh=mesh,
        in_specs=(P("stem", "tm", None), P(), P(), P(), P(), P(), P(), P(), P()),
        out_specs=P("stem", "tm", None),
        check_vma=False,
    )
```

profile of v0, /device:TPU:1, one launch (start us, length us, event | category | flops | bytes accessed | tf_op | source)
XLA Modules:
  0.0 176.1 jit_solution(18192869161088181082)
XLA Ops:
  6.5 2.2 %copy.46 = f32[50,6,1024]{2,1,0:T(8,128)S(1)} copy(f32[50,6,1024]{2,0,1:T(8,128)} %param.11) | data formatting | bytes 2457600 | tf_op args[2]
  9.0 1.9 %copy.75 = f32[7,8,6,1024]{3,1,2,0:T(8,128)} copy(f32[7,8,6,1024]{3,2,1,0:T(8,128)S(1)} %bitcast.95) | data formatting | bytes 2752512
  10.9 2.9 %dot_general.34 = f32[6,1024,50]{1,0,2:T(8,128)} reshape(f32[6144,50]{0,1:T(8,128)} %bitcast.97) | data formatting | bytes 2457600 | tf_op jit(solution)/shard_map/dot_general | solution.py:104
  13.8 1.3 convert_reduce_fusion.1
  15.1 1.5 fusion.17
  16.6 2.6 %fusion.23 = f32[8,6,1024]{2,0,1:T(8,128)S(1)} fusion(f32[6,1024,50]{1,0,2:T(8,128)} %dot_general.34, s32[8]{0:T(128)S(1)} %copy-done.10), kind=kOutput, calls=%fused_computation.35 | convolution fusion | flops 29491600 | bytes 1425440 | tf_op jit(solution)/shard_map/dot_general | solution.py:104
  19.3 1.5 fusion.20
  20.8 1.4 fusion.52
  24.3 5.2 %collective-permute-start.1 = (bf16[2,256,512]{1,2,0:T(8,128)(2,1)S(1)}, bf16[2,256,512]{1,2,0:T(8,128)(2,1)S(1)}, u32[]{:S(2)}, u32[]{:S(2)}) collective-permute-start(bf16[2,256,512]{1,2,0:T(8,128)(2,1)S(1)} %get-tuple-element.29), channel_id=1, source_target_pairs={{1,0},{2,1},{3,2},{4,3},{5,4},{6,5},{7,6},{8,7},{9,8},{10,9},{11,1... | collective-permute-start | bytes 1572872 | tf_op jit(solution)/shard_map/ppermute | solution.py:22
  29.4 3.2 %collective-permute-start = (bf16[2,256,512]{1,2,0:T(8,128)(2,1)S(1)}, bf16[2,256,512]{1,2,0:T(8,128)(2,1)}, u32[]{:S(2)}, u32[]{:S(2)}) collective-permute-start(bf16[2,256,512]{1,2,0:T(8,128)(2,1)S(1)} %get-tuple-element.28), channel_id=1, source_target_pairs={{0,1},{1,2},{2,3},{3,4},{4,5},{5,6},{6,7},{7,8},{8,9},{9,10},{10,1... | collective-permute-start | bytes 1572872 | tf_op jit(solution)/shard_map/ppermute | solution.py:19
  33.3 1.2 fusion.26
  34.6 8.5 %collective-permute-done.1 = bf16[2,256,512]{1,2,0:T(8,128)(2,1)S(1)} collective-permute-done((bf16[2,256,512]{1,2,0:T(8,128)(2,1)S(1)}, bf16[2,256,512]{1,2,0:T(8,128)(2,1)S(1)}, u32[]{:S(2)}, u32[]{:S(2)}) %collective-permute-start.1) | collective-permute-done | bytes 524320 | tf_op jit(solution)/shard_map/ppermute | solution.py:22
  43.0 1.2 pad_maximum_fusion
  45.4 9.1 %fusion.51 = (f32[8,384]{1,0:T(8,128)S(1)}, f32[8,384,896]{2,1,0:T(8,128)}) fusion(pred[384,896]{1,0:T(8,128)(4,1)S(1)} %copy-done.5, bf16[384,8,64]{0,2,1:T(8,128)(2,1)S(1)} %get-tuple-element.42, bf16[896,8,64]{0,2,1:T(8,128)(2,1)} %bitcast.105), kind=kOutput, calls=%fused_computation.98 | convolution fusion | flops 363332480 | bytes 12677120 | tf_op jit(solution)/shard_map/while/body/eval_jaxpr/sub | solution.py:56
  54.5 5.0 %divide_convert_fusion = bf16[8,384,896]{2,1,0:T(8,128)(2,1)S(1)} fusion(f32[8,384,896]{2,1,0:T(8,128)} %get-tuple-element.41, f32[8,384]{1,0:T(8,128)S(1)} %get-tuple-element.40), kind=kLoop, calls=%fused_computation.3 | loop fusion | flops 5505024 | bytes 16527360 | tf_op jit(solution)/shard_map/while/body/eval_jaxpr/convert_element_type | solution.py:28
  59.6 1.9 %convolution_convert_fusion.1 = bf16[8,64,384]{2,1,0:T(8,128)(2,1)S(1)} fusion(bf16[896,8,64]{0,2,1:T(8,128)(2,1)S(1)} %bitcast.98, bf16[8,384,896]{2,1,0:T(8,128)(2,1)S(1)} %divide_convert_fusion), kind=kOutput, calls=%fused_computation.40 | convolution fusion | flops 352518144 | bytes 6815744 | tf_op jit(solution)/shard_map/while/body/eval_jaxpr/hqk,khd->qhd/dot_general | solution.py:79
  64.3 1.4 fusion.53
  66.7 1.2 copy.54
  69.7 79.1 %all-gather.3.cloned.1.call-done = bf16[16,384,512]{2,1,0:T(8,128)(2,1)} async-done(((bf16[2,384,512]{2,1,0:T(8,128)(2,1)}), bf16[16,384,512]{2,1,0:T(8,128)(2,1)}) %all-gather.3.cloned.1.call-update) | async-done | bytes 6291472 | tf_op jit(solution)/shard_map/all_gather | solution.py:124
  148.7 6.1 %fusion.47 = (bf16[8,1,384,512]{3,2,1,0:T(8,128)(2,1)}, bf16[8,1,384,512]{3,2,1,0:T(8,128)(2,1)}) fusion(bf16[8,2,384,512]{3,2,1,0:T(8,128)(2,1)} %bitcast.96), kind=kLoop, calls=%fused_computation.94 | loop fusion | bytes 12582912 | tf_op jit(solution)/shard_map/slice | solution.py:125
  154.8 3.4 %copy.71 = bf16[8,1,384,512]{2,3,0,1:T(8,128)(2,1)S(1)} copy(bf16[8,1,384,512]{3,2,1,0:T(8,128)(2,1)} %get-tuple-element.14) | data formatting | bytes 6291456
  158.3 4.6 %copy.70 = bf16[8,1,384,512]{2,3,0,1:T(8,128)(2,1)} copy(bf16[8,1,384,512]{3,2,1,0:T(8,128)(2,1)} %get-tuple-element.13) | data formatting | bytes 6291456
  162.9 3.1 %multiply_reduce_fusion.1 = f32[384,8,8]{0,1,2:T(8,128)S(1)} fusion(bf16[384,8,64,8]{0,2,1,3:T(8,128)(2,1)} %bitcast.94, f32[384,8,64]{0,2,1:T(8,128)} %convert.8), kind=kLoop, calls=%fused_computation.8 | loop fusion | flops 4694016 | bytes 4030464
  168.1 1.2 fusion.33
  (75 shorter events, 11.5 us)
Async XLA Ops:
  6.5 14.2 %copy-start = (bf16[1024,1536]{1,0:T(8,128)(2,1)S(1)}, bf16[1024,1536]{1,0:T(8,128)(2,1)}, u32[]{:S(2)}) copy-start(bf16[1024,1536]{1,0:T(8,128)(2,1)} %param.12) | copy-start | bytes 9437188
  6.5 142.2 %all-gather.3.cloned.1.call-start = ((), (), s32[]{:S(2)}) async-start(), calls=%async_computation | async-start | bytes 7077888 | tf_op jit(solution)/shard_map/all_gather | solution.py:124
  10.9 5.7 %copy-start.10 = (s32[8]{0:T(128)S(1)}, s32[8]{0:T(128)}, u32[]{:S(2)}) copy-start(s32[8]{0:T(128)} %param.10) | copy-start | bytes 100
  22.2 0.7 copy-start.8
  24.0 8.8 %copy-start.9 = (f32[2,64]{1,0:T(2,128)S(1)}, f32[2,64]{1,0:T(2,128)}, u32[]{:S(2)}) copy-start(f32[2,64]{1,0:T(2,128)} %param.17) | copy-start | bytes 1540
  24.3 18.8 %collective-permute-start.1 = (bf16[2,256,512]{1,2,0:T(8,128)(2,1)S(1)}, bf16[2,256,512]{1,2,0:T(8,128)(2,1)S(1)}, u32[]{:S(2)}, u32[]{:S(2)}) collective-permute-start(bf16[2,256,512]{1,2,0:T(8,128)(2,1)S(1)} %get-tuple-element.29), channel_id=1, source_target_pairs={{1,0},{2,1},{3,2},{4,3},{5,4},{6,5},{7,6},{8,7},{9,8},{10,9},{11,1... | collective-permute-start | bytes 1572872 | tf_op jit(solution)/shard_map/ppermute | solution.py:22
  29.4 13.6 %collective-permute-start = (bf16[2,256,512]{1,2,0:T(8,128)(2,1)S(1)}, bf16[2,256,512]{1,2,0:T(8,128)(2,1)}, u32[]{:S(2)}, u32[]{:S(2)}) collective-permute-start(bf16[2,256,512]{1,2,0:T(8,128)(2,1)S(1)} %get-tuple-element.28), channel_id=1, source_target_pairs={{0,1},{1,2},{2,3},{3,4},{4,5},{5,6},{6,7},{7,8},{8,9},{9,10},{10,1... | collective-permute-start | bytes 1572872 | tf_op jit(solution)/shard_map/ppermute | solution.py:19
  44.3 1.1 copy-start.5
  59.5 1.9 %copy-start.4 = (bf16[1,384,1024]{2,1,0:T(8,128)(2,1)S(1)}, bf16[1,384,1024]{2,1,0:T(8,128)(2,1)}, u32[]{:S(2)}) copy-start(bf16[1,384,1024]{2,1,0:T(8,128)(2,1)} %param.9) | copy-start | bytes 2359300
  59.6 1.9 %copy-start.12 = (bf16[512,1024]{1,0:T(8,128)(2,1)S(1)}, bf16[512,1024]{1,0:T(8,128)(2,1)}, u32[]{:S(2)}) copy-start(bf16[512,1024]{1,0:T(8,128)(2,1)} %param.13) | copy-start | bytes 3145732
  62.1 0.9 copy-start.2
  62.1 2.2 %copy-start.11 = (bf16[1024,1536]{1,0:T(8,128)(2,1)S(1)}, bf16[1024,1536]{1,0:T(8,128)(2,1)}, u32[]{:S(2)}) copy-start(bf16[1024,1536]{1,0:T(8,128)(2,1)} %param.15) | copy-start | bytes 9437188
  65.9 0.6 copy-start.7
  67.9 0.7 copy-start.6
  166.1 1.2 copy-start.13
  166.9 1.2 copy-start.3
  166.9 2.4 %copy-start.1 = (bf16[1024,1536]{1,0:T(8,128)(2,1)S(1)}, bf16[1024,1536]{1,0:T(8,128)(2,1)}, u32[]{:S(2)}) copy-start(bf16[1024,1536]{1,0:T(8,128)(2,1)} %param.12) | copy-start | bytes 9437188
Sparse Core Ops, SparseCore 0:
  68.1 80.6 all-gather.2
where the time goes:
time: 177 us; the launch traced here: 176 us
  waiting for transfers between devices  87.6 us (49%)
  local copies, waits for them, and re-layouts  28.8 us (16%)
  other arithmetic  19.9 us (11%)
  matrix products  17.6 us (10%)
  between operations  13.9 us (8%)
  starting transfers between devices  8.4 us (5%)
    all_gather x1, waiting for transfers between devices, on_device(): every = lax.all_gather(pair, 'stem', axis=0, tiled=True)  79.1 us
    unnamed x34, local copies, waits for them, and re-layouts  15.1 us
    sub x1, matrix products, softmax_rows(): raised = jnp.exp(scores - top)  9.13 us
    ppermute x1, waiting for transfers between devices, padded_2(): lax.ppermute(lax.slice_in_dim(block, 0, width, axis=dim), axis, backward)  8.48 us
    convert_element_type x6, other arithmetic, rounded(): return lax.optimization_barrier(values.astype(jnp.bfloat16))  7.51 us
    slice x1, local copies, waits for them, and re-layouts, on_device(): k_all = every[:, 0].reshape(stem_count, rows, H, HD)  6.06 us
    ppermute x1, starting transfers between devices, padded_2(): lax.ppermute(lax.slice_in_dim(block, 0, width, axis=dim), axis, backward)  5.15 us
    unnamed x2, other arithmetic  4.04 us
  transfers between devices with their start and end apart: 3, of which 2 were waited for; matrix products, arithmetic and copies ran while one was open for 2% of the time, Pallas kernels for 0%

commit v1 on v0

--- a/solution.py
+++ b/solution.py
@@ -121,7 +121,8 @@
     projected_cross = jnp.dot(normed_cross, qkv_cross, preferred_element_type=jnp.float32)
     q_cross, k_cross, v_cross = split_heads(projected_cross, qk_gain_cross)
     pair = jnp.stack([k_cross.reshape(rows, width), v_cross.reshape(rows, width)])[None]
-    every = lax.all_gather(pair, "stem", axis=0, tiled=True)
+    outgoing = jnp.stack([pair] * lax.axis_size("stem"))
+    every = jnp.concatenate(lax.all_to_all(outgoing, "stem", 0, 0), axis=0)
     k_all = every[:, 0].reshape(stem_count, rows, H, HD)
     v_all = every[:, 1].reshape(stem_count, rows, H, HD)
     scores = jnp.einsum(

time: 177 us -> 151 us (0.85)
  the two profiles are of different devices: /device:TPU:1 before, /device:TPU:71 now
where the time goes in v1:
time: 151 us
  waiting for transfers between devices  79.3 us (53%)
  local copies, waits for them, and re-layouts  21.6 us (14%)
  other arithmetic  17.9 us (12%)
  matrix products  17.6 us (12%)
  starting transfers between devices  13.7 us (9%)
    all_to_all x1, waiting for transfers between devices, on_device(): every = jnp.concatenate(lax.all_to_all(outgoing, 'stem', 0, 0), axis=0)  69.6 us
    sub x1, matrix products, softmax_rows(): raised = jnp.exp(scores - top)  9.13 us
    ppermute x1, waiting for transfers between devices, padded_2(): lax.ppermute(lax.slice_in_dim(block, 0, width, axis=dim), axis, backward)  8.48 us
    convert_element_type x6, other arithmetic, rounded(): return lax.optimization_barrier(values.astype(jnp.bfloat16))  7.52 us
    unnamed x34, local copies, waits for them, and re-layouts  7.51 us
    ppermute x1, starting transfers between devices, padded_2(): lax.ppermute(lax.slice_in_dim(block, block.shape[dim] - width, None, axis...  6.19 us
    all_to_all x1, starting transfers between devices, on_device(): every = jnp.concatenate(lax.all_to_all(outgoing, 'stem', 0, 0), axis=0)  4.96 us
    all_to_all x1, local copies, waits for them, and re-layouts, on_device(): every = jnp.concatenate(lax.all_to_all(outgoing, 'stem', 0, 0), axis=0)  3.51 us
  transfers between devices with their start and end apart: 3, of which 3 were waited for; matrix products, arithmetic and copies ran while one was open for 2% of the time, Pallas kernels for 0%

profile of v1, /device:TPU:71, one launch (start us, length us, event | category | flops | bytes accessed | tf_op | source)
XLA Modules:
  0.0 150.6 jit_solution(2018885708322718750)
XLA Ops:
  0.0 2.2 %copy.33 = f32[50,6,1024]{2,1,0:T(8,128)S(1)} copy(f32[50,6,1024]{2,0,1:T(8,128)} %param.11) | data formatting | bytes 2457600 | tf_op args[2]
  2.5 1.9 %copy.58 = f32[7,8,6,1024]{3,1,2,0:T(8,128)} copy(f32[7,8,6,1024]{3,2,1,0:T(8,128)S(1)} %bitcast.96) | data formatting | bytes 2752512
  4.4 2.9 %dot_general.34 = f32[6,1024,50]{1,0,2:T(8,128)} reshape(f32[6144,50]{0,1:T(8,128)} %bitcast.97) | data formatting | bytes 2457600 | tf_op jit(solution)/shard_map/dot_general | solution.py:104
  7.3 1.3 convert_reduce_fusion.1
  8.6 1.5 fusion.17
  10.1 2.6 %fusion.23 = f32[8,6,1024]{2,0,1:T(8,128)S(1)} fusion(f32[6,1024,50]{1,0,2:T(8,128)} %dot_general.34, s32[8]{0:T(128)S(1)} %copy-done.11), kind=kOutput, calls=%fused_computation.36 | convolution fusion | flops 29491600 | bytes 1425440 | tf_op jit(solution)/shard_map/dot_general | solution.py:104
  12.7 1.5 fusion.20
  14.3 1.4 fusion.52
  17.7 2.6 %collective-permute-start.1 = (bf16[2,256,512]{1,2,0:T(8,128)(2,1)S(1)}, bf16[2,256,512]{1,2,0:T(8,128)(2,1)S(1)}, u32[]{:S(2)}, u32[]{:S(2)}) collective-permute-start(bf16[2,256,512]{1,2,0:T(8,128)(2,1)S(1)} %get-tuple-element.29), channel_id=1, source_target_pairs={{1,0},{2,1},{3,2},{4,3},{5,4},{6,5},{7,6},{8,7},{9,8},{10,9},{11,1... | collective-permute-start | bytes 1572872 | tf_op jit(solution)/shard_map/ppermute | solution.py:22
  20.3 6.2 %collective-permute-start = (bf16[2,256,512]{1,2,0:T(8,128)(2,1)S(1)}, bf16[2,256,512]{1,2,0:T(8,128)(2,1)}, u32[]{:S(2)}, u32[]{:S(2)}) collective-permute-start(bf16[2,256,512]{1,2,0:T(8,128)(2,1)S(1)} %get-tuple-element.28), channel_id=1, source_target_pairs={{0,1},{1,2},{2,3},{3,4},{4,5},{5,6},{6,7},{7,8},{8,9},{9,10},{10,1... | collective-permute-start | bytes 1572872 | tf_op jit(solution)/shard_map/ppermute | solution.py:19
  27.2 1.2 fusion.26
  28.4 8.5 %collective-permute-done.1 = bf16[2,256,512]{1,2,0:T(8,128)(2,1)S(1)} collective-permute-done((bf16[2,256,512]{1,2,0:T(8,128)(2,1)S(1)}, bf16[2,256,512]{1,2,0:T(8,128)(2,1)S(1)}, u32[]{:S(2)}, u32[]{:S(2)}) %collective-permute-start.1) | collective-permute-done | bytes 524320 | tf_op jit(solution)/shard_map/ppermute | solution.py:22
  36.9 1.1 collective-permute-done
  38.0 1.2 pad_maximum_fusion
  40.3 9.1 %fusion.51 = (f32[8,384]{1,0:T(8,128)S(1)}, f32[8,384,896]{2,1,0:T(8,128)}) fusion(pred[384,896]{1,0:T(8,128)(4,1)S(1)} %copy-done.6, bf16[384,8,64]{0,2,1:T(8,128)(2,1)S(1)} %get-tuple-element.42, bf16[896,8,64]{0,2,1:T(8,128)(2,1)} %bitcast.105), kind=kOutput, calls=%fused_computation.99 | convolution fusion | flops 363332480 | bytes 12677120 | tf_op jit(solution)/shard_map/while/body/eval_jaxpr/sub | solution.py:56
  49.5 5.0 %divide_convert_fusion = bf16[8,384,896]{2,1,0:T(8,128)(2,1)S(1)} fusion(f32[8,384,896]{2,1,0:T(8,128)} %get-tuple-element.41, f32[8,384]{1,0:T(8,128)S(1)} %get-tuple-element.40), kind=kLoop, calls=%fused_computation.3 | loop fusion | flops 5505024 | bytes 16527360 | tf_op jit(solution)/shard_map/while/body/eval_jaxpr/convert_element_type | solution.py:28
  54.5 1.9 %convolution_convert_fusion.1 = bf16[8,64,384]{2,1,0:T(8,128)(2,1)S(1)} fusion(bf16[896,8,64]{0,2,1:T(8,128)(2,1)S(1)} %bitcast.98, bf16[8,384,896]{2,1,0:T(8,128)(2,1)S(1)} %divide_convert_fusion), kind=kOutput, calls=%fused_computation.41 | convolution fusion | flops 352518144 | bytes 6815744 | tf_op jit(solution)/shard_map/while/body/eval_jaxpr/hqk,khd->qhd/dot_general | solution.py:79
  58.0 1.2 copy-done.12
  59.2 1.4 fusion.53
  61.8 3.5 %stack.11 = bf16[8,1,2,384,512]{3,4,2,1,0:T(8,128)(2,1)} broadcast(bf16[2,384,512]{1,2,0:T(8,128)(2,1)S(1)} %pad_maximum_fusion.1), dimensions={2,3,4} | broadcast | bytes 7077888 | tf_op jit(solution)/shard_map/stack | solution.py:124
  65.2 5.0 %all-to-all-start = ((bf16[8,1,2,384,512]{3,4,2,1,0:T(8,128)(2,1)}), bf16[8,1,2,384,512]{3,4,2,1,0:T(8,128)(2,1)}, u32[]{:S(2)}, u32[]{:S(2)}) async-start(bf16[8,1,2,384,512]{3,4,2,1,0:T(8,128)(2,1)} %stack.11), calls=%async_computation | async-start | bytes 12582912 | tf_op jit(solution)/shard_map/all_to_all | solution.py:125
  72.0 69.6 %all-to-all-done = bf16[8,1,2,384,512]{3,4,2,1,0:T(8,128)(2,1)} async-done(((bf16[8,1,2,384,512]{3,4,2,1,0:T(8,128)(2,1)}), bf16[8,1,2,384,512]{3,4,2,1,0:T(8,128)(2,1)}, u32[]{:S(2)}, u32[]{:S(2)}) %all-to-all-start) | async-done | bytes 6291488 | tf_op jit(solution)/shard_map/all_to_all | solution.py:125
  141.6 3.5 %copy.68 = bf16[8,1,2,384,512]{3,4,0,2,1:T(8,128)(2,1)S(1)} copy(bf16[8,1,2,384,512]{3,4,2,1,0:T(8,128)(2,1)} %all-to-all-done) | data formatting | bytes 12582912 | tf_op jit(solution)/shard_map/all_to_all | solution.py:125
  149.4 1.2 fusion.33
  (75 shorter events, 12.5 us)
Async XLA Ops:
  0.0 14.2 %copy-start = (bf16[1024,1536]{1,0:T(8,128)(2,1)S(1)}, bf16[1024,1536]{1,0:T(8,128)(2,1)}, u32[]{:S(2)}) copy-start(bf16[1024,1536]{1,0:T(8,128)(2,1)} %param.12) | copy-start | bytes 9437188
  4.4 5.7 %copy-start.11 = (s32[8]{0:T(128)S(1)}, s32[8]{0:T(128)}, u32[]{:S(2)}) copy-start(s32[8]{0:T(128)} %param.10) | copy-start | bytes 100
  15.6 0.7 copy-start.9
  17.4 9.2 %copy-start.10 = (f32[2,64]{1,0:T(2,128)S(1)}, f32[2,64]{1,0:T(2,128)}, u32[]{:S(2)}) copy-start(f32[2,64]{1,0:T(2,128)} %param.17) | copy-start | bytes 1540
  17.7 19.1 %collective-permute-start.1 = (bf16[2,256,512]{1,2,0:T(8,128)(2,1)S(1)}, bf16[2,256,512]{1,2,0:T(8,128)(2,1)S(1)}, u32[]{:S(2)}, u32[]{:S(2)}) collective-permute-start(bf16[2,256,512]{1,2,0:T(8,128)(2,1)S(1)} %get-tuple-element.29), channel_id=1, source_target_pairs={{1,0},{2,1},{3,2},{4,3},{5,4},{6,5},{7,6},{8,7},{9,8},{10,9},{11,1... | collective-permute-start | bytes 1572872 | tf_op jit(solution)/shard_map/ppermute | solution.py:22
  20.3 17.7 %collective-permute-start = (bf16[2,256,512]{1,2,0:T(8,128)(2,1)S(1)}, bf16[2,256,512]{1,2,0:T(8,128)(2,1)}, u32[]{:S(2)}, u32[]{:S(2)}) collective-permute-start(bf16[2,256,512]{1,2,0:T(8,128)(2,1)S(1)} %get-tuple-element.28), channel_id=1, source_target_pairs={{0,1},{1,2},{2,3},{3,4},{4,5},{5,6},{6,7},{7,8},{8,9},{9,10},{10,1... | collective-permute-start | bytes 1572872 | tf_op jit(solution)/shard_map/ppermute | solution.py:19
  39.2 1.1 copy-start.6
  54.5 1.9 %copy-start.4 = (bf16[1,384,1024]{2,1,0:T(8,128)(2,1)S(1)}, bf16[1,384,1024]{2,1,0:T(8,128)(2,1)}, u32[]{:S(2)}) copy-start(bf16[1,384,1024]{2,1,0:T(8,128)(2,1)} %param.9) | copy-start | bytes 2359300
  54.5 1.9 %copy-start.13 = (bf16[512,1024]{1,0:T(8,128)(2,1)S(1)}, bf16[512,1024]{1,0:T(8,128)(2,1)}, u32[]{:S(2)}) copy-start(bf16[512,1024]{1,0:T(8,128)(2,1)} %param.13) | copy-start | bytes 3145732
  57.1 3.6 %copy-start.2 = (bf16[384,1024]{1,0:T(8,128)(2,1)}, bf16[384,1024]{1,0:T(8,128)(2,1)S(1)}, u32[]{:S(2)}) copy-start(bf16[384,1024]{1,0:T(8,128)(2,1)S(1)} %fusion.21) | copy-start | bytes 2359300
  57.1 2.2 %copy-start.12 = (bf16[1024,1536]{1,0:T(8,128)(2,1)S(1)}, bf16[1024,1536]{1,0:T(8,128)(2,1)}, u32[]{:S(2)}) copy-start(bf16[1024,1536]{1,0:T(8,128)(2,1)} %param.15) | copy-start | bytes 9437188
  60.8 0.7 copy-start.8
  65.2 76.4 %all-to-all-start = ((bf16[8,1,2,384,512]{3,4,2,1,0:T(8,128)(2,1)}), bf16[8,1,2,384,512]{3,4,2,1,0:T(8,128)(2,1)}, u32[]{:S(2)}, u32[]{:S(2)}) async-start(bf16[8,1,2,384,512]{3,4,2,1,0:T(8,128)(2,1)} %stack.11), calls=%async_computation | async-start | bytes 12582912 | tf_op jit(solution)/shard_map/all_to_all | solution.py:125
  70.2 0.7 copy-start.7
  145.1 1.1 copy-start.5
  147.4 1.2 copy-start.14
  148.2 1.2 copy-start.3
  148.2 2.4 %copy-start.1 = (bf16[1024,1536]{1,0:T(8,128)(2,1)S(1)}, bf16[1024,1536]{1,0:T(8,128)(2,1)}, u32[]{:S(2)}) copy-start(bf16[1024,1536]{1,0:T(8,128)(2,1)} %param.12) | copy-start | bytes 9437188
